TPU v7x, 256 devices: a whole 4x4x8 slice. The times are simulated.
256 devices in a mesh: grp: 8 (over z_lo, core), dev: 32 (over z_hi, x, y).
Axes of the slice: x: 4, y: 4, z: 8 (z_hi: 2, z_lo: 4; z = z_hi * 4 + z_lo), core: 2. Of those that a mesh axis runs over, the one named last changes fastest.
Arguments:
- images: bfloat16 [131072, 64, 128], P(('grp', 'dev')), may hold values from -16 to 16
- test_maps: bfloat16 [64, 128, 32], replicated, may hold values from -6 to 6
- counts: int32 [64], replicated, may hold values from 24 to 64, as said below
Outputs:
- projected: bfloat16 [131072, 64, 32], P(('grp', 'dev'))
Inputs may be any that keep to these rules, and one draw needn't show every extreme that they name: `counts`: block 0 has 64 radial functions and block 63 has 24.
All inputs are finite; a program needn't handle non-finite values.
Results may differ from a plain program's by a relative error of at most 0.0049.
Values may be sent and summed in bfloat16 or wider, within the bound.
No kernel may reach another device: no remote copies, remote signals or barrier semaphores. Data moves between devices by JAX's collectives and lax.ppermute only.
A program may use at most 64 MiB of HBM per device.

v0:
```python
import jax
import jax.numpy as jnp
from jax import lax
from jax.sharding import PartitionSpec as P


def orthonormal(summed):
    gram_matrix = jnp.einsum("krs,krt->kst", summed, summed, precision=lax.Precision.HIGHEST)
    factor = jnp.linalg.cholesky(gram_matrix)
    solved = lax.linalg.triangular_solve(
        factor, summed, left_side=False, lower=True, transpose_a=True
    )
    return solved.astype(jnp.bfloat16)


def body(images, test_maps, counts):
    columns = images.shape[2]
    radial = columns // 2
    position = lax.broadcasted_iota(jnp.int32, (images.shape[1], columns), 1) % radial
    valid_mask = (position < counts[:, None]).astype(jnp.bfloat16)
    masked = images * valid_mask[None]
    sketch = jnp.einsum(
        "ikr,krs->iks", masked, test_maps, preferred_element_type=jnp.float32
    ).astype(jnp.bfloat16)
    partial_sum = jnp.einsum("ikr,iks->krs", masked, sketch, preferred_element_type=jnp.float32)
    totals = lax.psum(partial_sum, "grp")
    owned = lax.psum_scatter(totals, "dev", scatter_dimension=0, tiled=True)
    basis_all = lax.all_gather(orthonormal(owned), "dev", axis=0, tiled=True)
    projected = jnp.einsum("ikr,krs->iks", masked, basis_all, preferred_element_type=jnp.float32)
    return projected.astype(jnp.bfloat16)


def solution(mesh):
    in_specs = (P(("grp", "dev"), None, None), P(), P())
    out_specs = P(("grp", "dev"), None, None)
    return jax.shard_map(body, mesh=mesh, in_specs=in_specs, out_specs=out_specs, check_vma=False)
```

profile of v0, /device:TPU:8, one launch (start us, length us, event | category | flops | bytes accessed | tf_op | source)
XLA Modules:
  0.0 447.4 jit_solution(9453604602450856554)
XLA Ops:
  6.5 0.0 copy-start
  6.5 0.0 reduce-scatter.2.cloned.1.call-start
  6.5 0.8 fusion.16
  7.3 7.2 %broadcast_multiply_fusion = bf16[512,64,128]{2,1,0:T(8,128)(2,1)} fusion(bf16[512,64,128]{2,1,0:T(8,128)(2,1)} %param.3, bf16[64,128]{1,0:T(8,128)(2,1)S(1)} %fusion.16), kind=kLoop, calls=%fused_computation.6 | loop fusion | flops 4194304 | bytes 16793600 | tf_op jit(solution)/shard_map/mul | solution.py:21
  14.5 0.0 copy-done
  14.5 24.3 %fusion.4 = f32[64,128,32]{1,2,0:T(8,128)} fusion(bf16[512,64,128]{2,1,0:T(8,128)(2,1)} %broadcast_multiply_fusion, bf16[64,128,32]{1,2,0:T(8,128)(2,1)S(1)} %copy-done), kind=kOutput, calls=%fused_computation.4 | convolution fusion | flops 537919488 | bytes 9961472 | tf_op jit(solution)/shard_map/ikr,iks->krs/dot_general | solution.py:25
  38.8 0.0 reduce-scatter.2.cloned.1.call-update
  38.9 222.5 %reduce-scatter.2.cloned.1.call-done = f32[2,128,32]{1,2,0:T(8,128)} async-done(((f32[64,128,32]{1,2,0:T(8,128)}), f32[2,128,32]{1,2,0:T(8,128)}) %reduce-scatter.2.cloned.1.call-update) | async-done | bytes 32784 | tf_op jit(solution)/shard_map/reduce_scatter | solution.py:27
  261.4 26.5 %psum.8 = f32[2,128,32]{1,2,0:T(8,128)S(1)} all-reduce(f32[2,128,32]{1,2,0:T(8,128)} %reduce-scatter.2.cloned.1.call-done), channel_id=1, replica_groups=mesh['grp'=8,'dev'=32] {'grp'}, use_global_device_ids=true, to_apply=%region_0.1 | all-reduce | flops 8192 | bytes 65536 | tf_op jit(solution)/shard_map/psum | solution.py:26
  287.9 0.2 fusion.17
  288.1 0.1 copy.12
  288.2 5.9 %custom-call.7 = f32[2,32,32]{2,1,0:T(8,128)S(1)} custom-call(f32[2,32,32]{2,1,0:T(8,128)S(1)} %fusion.15), custom_call_target="Cholesky" | custom-call | tf_op jit(solution)/shard_map/jit(cholesky)/cholesky | solution.py:9
  294.1 0.1 compare_reduce_fusion
  294.2 0.1 select_bitcast_fusion
  294.3 4.9 %custom-call.8 = f32[2,1,32,32]{2,3,1,0:T(8,128)S(1)} custom-call(f32[2,1,32,32]{3,2,1,0:T(8,128)S(1)} %select_bitcast_fusion), custom_call_target="InvertDiagBlocksLowerTriangular" | custom-call | tf_op jit(solution)/shard_map/triangular_solve | solution.py:10
  299.2 0.3 convolution_convert_fusion
  299.4 119.3 %all_gather.3 = bf16[64,128,32]{1,2,0:T(8,128)(2,1)S(1)} all-gather(bf16[2,128,32]{1,2,0:T(8,128)(2,1)S(1)} %convolution_convert_fusion), channel_id=1, replica_groups=mesh['grp'=8,'dev'=32] {'dev'}, dimensions={0}, use_global_device_ids=true | all-gather | bytes 540672 | tf_op jit(solution)/shard_map/all_gather | solution.py:28
  418.8 21.8 %convert_bitcast_fusion = bf16[512,64,32]{0,2,1:T(8,128)(2,1)} fusion(bf16[64,128,32]{1,2,0:T(8,128)(2,1)S(1)} %all_gather.3, bf16[512,64,128]{2,1,0:T(8,128)(2,1)} %broadcast_multiply_fusion), kind=kOutput, calls=%fused_computation.8 | convolution fusion | flops 269484032 | bytes 11010048 | tf_op jit(solution)/shard_map/ikr,krs->iks/dot_general | solution.py:29
  (6 shorter events, 0.1 us)
Async XLA Ops:
  6.5 8.0 %copy-start = (bf16[64,128,32]{1,2,0:T(8,128)(2,1)S(1)}, bf16[64,128,32]{1,2,0:T(8,128)(2,1)}, u32[]{:S(2)}) copy-start(bf16[64,128,32]{1,2,0:T(8,128)(2,1)} %param.4) | copy-start | bytes 1572868
  6.5 254.9 %reduce-scatter.2.cloned.1.call-start = ((), (), s32[]{:S(2)}) async-start(), calls=%async_computation.1 | async-start | bytes 1081344 | tf_op jit(solution)/shard_map/reduce_scatter | solution.py:27
Sparse Core Ops, SparseCore 0:
  39.0 222.4 reduce-scatter.1
where the time goes:
time: 448 us; the launch traced here: 447 us
  waiting for transfers between devices  223 us (50%)
  blocking collectives  146 us (33%)
  matrix products  46.5 us (10%)
  other arithmetic  19 us (4%)
  between operations  13.4 us (3%)
    reduce_scatter x1, waiting for transfers between devices, body(): owned = lax.psum_scatter(totals, 'dev', scatter_dimension=0, tiled=True)  223 us
    all_gather x1, blocking collectives, body(): basis_all = lax.all_gather(orthonormal(owned), 'dev', axis=0, tiled=True)  119 us
    psum x1, blocking collectives, body(): totals = lax.psum(partial_sum, 'grp')  26.5 us
    dot_general x1, matrix products, body(): jnp.einsum('ikr,iks->krs', masked, sketch, preferred_element_type=jnp.flo...  24.3 us
    dot_general x1, matrix products, body(): jnp.einsum('ikr,krs->iks', masked, basis_all, preferred_element_type=jnp....  21.8 us
  transfers between devices with their start and end apart: 1, of which 1 were waited for; matrix products, arithmetic and copies ran while one was open for 0% of the time, Pallas kernels for 0%

commit v1 on v0

--- a/solution.py
+++ b/solution.py
@@ -25,7 +25,9 @@
     partial_sum = jnp.einsum("ikr,iks->krs", masked, sketch, preferred_element_type=jnp.float32)
     totals = lax.psum(partial_sum, "grp")
     owned = lax.psum_scatter(totals, "dev", scatter_dimension=0, tiled=True)
-    basis_all = lax.all_gather(orthonormal(owned), "dev", axis=0, tiled=True)
+    basis_all = jnp.concatenate(
+        lax.all_to_all(jnp.stack([orthonormal(owned)] * lax.axis_size("dev")), "dev", 0, 0), axis=0
+    )
     projected = jnp.einsum("ikr,krs->iks", masked, basis_all, preferred_element_type=jnp.float32)
     return projected.astype(jnp.bfloat16)
 

time: 448 us -> 355 us (0.79)
  blocking collectives: 146 us -> 53 us
    all_gather x1 -> x0, blocking collectives: 119 us -> none  [body(): basis_all = lax.all_gather(orthonormal(owned), 'dev', axis=0, tiled=True)]
    all_to_all x0 -> x1, blocking collectives: none -> 26.5 us  [body(): lax.all_to_all(jnp.stack([orthonormal(owned)] * lax.axis_size('dev')), 'd...]
where the time goes in v1:
time: 355 us
  waiting for transfers between devices  223 us (63%)
  blocking collectives  53 us (15%)
  matrix products  46.5 us (13%)
  other arithmetic  19 us (5%)
  between operations  13.4 us (4%)
    reduce_scatter x1, waiting for transfers between devices, body(): owned = lax.psum_scatter(totals, 'dev', scatter_dimension=0, tiled=True)  223 us
    all_to_all x1, blocking collectives, body(): lax.all_to_all(jnp.stack([orthonormal(owned)] * lax.axis_size('dev')), 'd...  26.5 us
    psum x1, blocking collectives, body(): totals = lax.psum(partial_sum, 'grp')  26.5 us
    dot_general x1, matrix products, body(): jnp.einsum('ikr,iks->krs', masked, sketch, preferred_element_type=jnp.flo...  24.3 us
    dot_general x1, matrix products, body(): jnp.einsum('ikr,krs->iks', masked, basis_all, preferred_element_type=jnp....  21.8 us
    mul x1, other arithmetic, body(): masked = images * valid_mask[None]  7.16 us
  transfers between devices with their start and end apart: 1, of which 1 were waited for; matrix products, arithmetic and copies ran while one was open for 0% of the time, Pallas kernels for 0%

profile of v1, /device:TPU:8, one launch (start us, length us, event | category | flops | bytes accessed | tf_op | source)
XLA Modules:
  0.0 354.7 jit_solution(4509491801229491688)
XLA Ops:
  6.5 0.0 copy-start
  6.5 0.0 reduce-scatter.2.cloned.1.call-start
  6.5 0.8 fusion.16
  7.3 7.2 %broadcast_multiply_fusion = bf16[512,64,128]{2,1,0:T(8,128)(2,1)} fusion(bf16[512,64,128]{2,1,0:T(8,128)(2,1)} %param.3, bf16[64,128]{1,0:T(8,128)(2,1)S(1)} %fusion.16), kind=kLoop, calls=%fused_computation.6 | loop fusion | flops 4194304 | bytes 16793600 | tf_op jit(solution)/shard_map/mul | solution.py:21
  14.5 0.0 copy-done
  14.5 24.3 %fusion.4 = f32[64,128,32]{1,2,0:T(8,128)} fusion(bf16[512,64,128]{2,1,0:T(8,128)(2,1)} %broadcast_multiply_fusion, bf16[64,128,32]{1,2,0:T(8,128)(2,1)S(1)} %copy-done), kind=kOutput, calls=%fused_computation.4 | convolution fusion | flops 537919488 | bytes 9961472 | tf_op jit(solution)/shard_map/ikr,iks->krs/dot_general | solution.py:25
  38.8 0.0 reduce-scatter.2.cloned.1.call-update
  38.9 222.5 %reduce-scatter.2.cloned.1.call-done = f32[2,128,32]{1,2,0:T(8,128)} async-done(((f32[64,128,32]{1,2,0:T(8,128)}), f32[2,128,32]{1,2,0:T(8,128)}) %reduce-scatter.2.cloned.1.call-update) | async-done | bytes 32784 | tf_op jit(solution)/shard_map/reduce_scatter | solution.py:27
  261.4 26.5 %psum.8 = f32[2,128,32]{1,2,0:T(8,128)S(1)} all-reduce(f32[2,128,32]{1,2,0:T(8,128)} %reduce-scatter.2.cloned.1.call-done), channel_id=1, replica_groups=mesh['grp'=8,'dev'=32] {'grp'}, use_global_device_ids=true, to_apply=%region_0.1 | all-reduce | flops 8192 | bytes 65536 | tf_op jit(solution)/shard_map/psum | solution.py:26
  287.9 0.2 fusion.17
  288.1 0.1 copy.9
  288.2 5.9 %custom-call.7 = f32[2,32,32]{2,1,0:T(8,128)S(1)} custom-call(f32[2,32,32]{2,1,0:T(8,128)S(1)} %fusion.15), custom_call_target="Cholesky" | custom-call | tf_op jit(solution)/shard_map/jit(cholesky)/cholesky | solution.py:9
  294.1 0.1 compare_reduce_fusion
  294.2 0.1 select_bitcast_fusion
  294.3 4.9 %custom-call.8 = f32[2,1,32,32]{2,3,1,0:T(8,128)S(1)} custom-call(f32[2,1,32,32]{3,2,1,0:T(8,128)S(1)} %select_bitcast_fusion), custom_call_target="InvertDiagBlocksLowerTriangular" | custom-call | tf_op jit(solution)/shard_map/triangular_solve | solution.py:10
  299.2 0.3 convolution_convert_fusion
  299.4 0.1 stack.2
  299.6 26.5 %all_to_all.5 = bf16[32,2,128,32]{2,3,1,0:T(8,128)(2,1)S(1)} all-to-all(bf16[32,2,128,32]{2,3,1,0:T(8,128)(2,1)S(1)} %stack.2), channel_id=1, replica_groups=mesh['grp'=8,'dev'=32] {'dev'}, dimensions={0} | all-to-all | bytes 1048576 | tf_op jit(solution)/shard_map/all_to_all | solution.py:29
  326.1 21.8 %convert_bitcast_fusion = bf16[512,64,32]{0,2,1:T(8,128)(2,1)} fusion(bf16[64,128,32]{1,2,0:T(8,128)(2,1)S(1)} %bitcast.20, bf16[512,64,128]{2,1,0:T(8,128)(2,1)} %broadcast_multiply_fusion), kind=kOutput, calls=%fused_computation.8 | convolution fusion | flops 269484032 | bytes 11010048 | tf_op jit(solution)/shard_map/ikr,krs->iks/dot_general | solution.py:31
  (6 shorter events, 0.1 us)
Async XLA Ops:
  6.5 8.0 %copy-start = (bf16[64,128,32]{1,2,0:T(8,128)(2,1)S(1)}, bf16[64,128,32]{1,2,0:T(8,128)(2,1)}, u32[]{:S(2)}) copy-start(bf16[64,128,32]{1,2,0:T(8,128)(2,1)} %param.4) | copy-start | bytes 1572868
  6.5 254.9 %reduce-scatter.2.cloned.1.call-start = ((), (), s32[]{:S(2)}) async-start(), calls=%async_computation.2 | async-start | bytes 1081344 | tf_op jit(solution)/shard_map/reduce_scatter | solution.py:27
Sparse Core Ops, SparseCore 0:
  39.0 222.4 reduce-scatter.1
